TPU v7x, 32 devices: a whole 2x2x4 slice. The times are simulated.
32 devices in a mesh: groups: 2 (over y), blk: 4 (over z), leaf: 2 (over x), sample: 2 (over core).
Axes of the slice: x: 2, y: 2, z: 4, core: 2. Of those that a mesh axis runs over, the one named last changes fastest.
Arguments:
- residual: float32 [256, 128, 256], P(('groups', 'blk', 'leaf'), 'sample'), parts along dimension 0, may hold values from -60 to 60
- direction: bfloat16 [256, 128, 256], P(('groups', 'blk', 'leaf'), 'sample'), parts along dimension 0, may hold values from -60 to 60
- step: float32 [256], P(('groups', 'sample')), parts along dimension 0, may hold values from 0.2 to 0.8
- coords: bfloat16 [256, 3, 256], P(('groups', 'blk', 'leaf')), parts along dimension 0, may hold values from 0 to 1
- order: int32 [256, 256], P(('groups', 'blk', 'leaf')), parts along dimension 0, may hold values from 0 to 255, each once within a row
- basis: bfloat16 [256, 64, 256], P(('groups', 'blk', 'leaf')), parts along dimension 0, may hold values from -0.5 to 0.5
- leaf_transfer: bfloat16 [256, 64, 64], P(('groups', 'blk', 'leaf')), parts along dimension 0, may hold values from -0.75 to 0.75
- node_transfer: bfloat16 [16, 64, 64], P(('groups', 'blk', 'leaf')), parts along dimension 0, may hold values from -0.75 to 0.75
- near_list: int32 [256, 12], P(('groups', 'blk', 'leaf')), parts along dimension 0, may hold values from 0 to 127, as said below
- coupling_list: int32 [256, 8], P(('groups', 'blk', 'leaf')), parts along dimension 0, may hold values from 0 to 127, as said below
- coupling: bfloat16 [256, 8, 64, 64], P(('groups', 'blk', 'leaf')), parts along dimension 0, may hold values from -0.25 to 0.25
- top_list: int32 [8, 4], P(('groups', 'blk')), parts along dimension 0, may hold values from 0 to 3, as said below
- top_coupling: bfloat16 [8, 4, 64, 64], P(('groups', 'blk')), parts along dimension 0, may hold values from -0.0625 to 0.0625
Outputs:
- residual_next: float32 [256, 128, 256], P(('groups', 'blk', 'leaf'), 'sample'), parts along dimension 0
- direction_next: bfloat16 [256, 128, 256], P(('groups', 'blk', 'leaf'), 'sample'), parts along dimension 0
There are 2 independent parts, one for each index of `groups`. A program takes and returns all parts, laid end to end along the dimension named above; each array names one. Nothing has to cross between parts.
Inputs may be any that keep to these rules, and one draw needn't show every extreme that they name: `near_list`: entry 0 of leaf g is g itself; the other entries are distinct leaves other than g, each at most 16 positions from g around the cycle of 128 leaves; some leaf names both g - 16 and g + 16 (mod 128). `coupling_list`: the entries of leaf g are distinct leaves of the aligned blocks of 16 leaves just before and just after g's own block, around the cycle of 128 leaves, each more than 16 positions from g. `top_list`: the entries of top cluster b name clusters other than b; they may repeat.
All inputs are finite; a program needn't handle non-finite values.
Results may differ from a plain program's by a relative error of at most 0.0065.
Values may be sent and summed in bfloat16 or wider, within the bound.
No kernel may reach another device: no remote copies, remote signals or barrier semaphores. Data moves between devices by JAX's collectives and lax.ppermute only.
A program may use at most 64 MiB of HBM per device.

v0:
```python
import math
import jax
import jax.numpy as jnp
from jax import lax
from jax.sharding import PartitionSpec as P

LEAF_DEV = 16
ROOT_THREE = math.sqrt(3.0)
LENGTH = 0.3
AMPLITUDE = 0.25
NUGGET = 0.5


def padded(array, sides, width):
    for axis, dim in sides:
        count, length = (lax.axis_size(axis), array.shape[dim])
        up = [(i, (i + 1) % count) for i in range(count)]
        down = [(j, i) for i, j in up]
        last = lax.slice_in_dim(array, length - width, length, axis=dim)
        initial = lax.slice_in_dim(array, 0, width, axis=dim)
        before = lax.ppermute(last, axis, up)
        after = lax.ppermute(initial, axis, down)
        array = jnp.concatenate([before, array, after], axis=dim)
    return array


def swapped(array, axis, bit):
    return lax.ppermute(array, axis, [(i, i ^ 1 << bit) for i in range(lax.axis_size(axis))])


def matern(own_offsets, near_offsets, gap_leaves, spread):
    gap_x = (
        own_offsets[0][:, None] - near_offsets[0][None, :] + gap_leaves.astype(jnp.float32) * spread
    )
    gap_y = own_offsets[1][:, None] - near_offsets[1][None, :]
    gap_z = own_offsets[2][:, None] - near_offsets[2][None, :]
    scaled = jnp.sqrt(gap_x * gap_x + gap_y * gap_y + gap_z * gap_z) * (ROOT_THREE / LENGTH)
    return AMPLITUDE * (1.0 + scaled) * jnp.exp(-scaled)


def tile_block(own_offsets, near_offsets, gap_leaves, spread):
    inner = jax.vmap(matern, in_axes=(None, 0, 0, None))
    return jax.vmap(inner, in_axes=(0, 0, 0, None))(own_offsets, near_offsets, gap_leaves, spread)


def on_device(
    residual,
    direction,
    step,
    coords,
    order,
    basis,
    leaf_transfer,
    node_transfer,
    near_list,
    coupling_list,
    coupling,
    top_list,
    top_coupling,
):
    leaf_dev = direction.shape[0]
    samples = direction.shape[1]
    points = direction.shape[2]
    blk_count = lax.axis_size("blk")
    leaf_count = lax.axis_size("leaf")
    leaf_total = leaf_dev * blk_count * leaf_count
    device = lax.axis_index("blk") * leaf_count + lax.axis_index("leaf")
    first_leaf = device * leaf_dev
    spread = 0.5 / LEAF_DEV
    old_norm = lax.psum(jnp.sum(residual * residual, axis=(0, 2)), ("blk", "leaf"))
    packed = jnp.concatenate([direction, coords], axis=1)
    widened = padded(packed, ((("blk", "leaf"), 0),), leaf_dev)
    anchor = first_leaf - leaf_dev
    own_offsets_all = coords.astype(jnp.float32)
    slot_ids = jnp.mod(near_list - anchor, leaf_total)
    window_values = widened[:, :samples, :]
    window_offsets = widened[:, samples:, :]
    half_rows = leaf_dev // 2
    side = lax.axis_index("sample")
    partner_values = swapped(window_values, "sample", 0)
    all_columns = jnp.where(
        side == 0,
        jnp.concatenate([window_values, partner_values], axis=1),
        jnp.concatenate([partner_values, window_values], axis=1),
    )
    base = side * half_rows
    blocks = 4
    columns = all_columns.shape[1]

    def near_block(block_index):
        start_at = base + block_index * blocks
        slot_rows = lax.dynamic_slice_in_dim(slot_ids, start_at, blocks, 0)
        name_rows = lax.dynamic_slice_in_dim(near_list, start_at, blocks, 0)
        leaf_ids = first_leaf + start_at + jnp.arange(blocks, dtype=jnp.int32)
        near_values = all_columns[slot_rows]
        near_offsets = window_offsets[slot_rows].astype(jnp.float32)
        own_offsets = lax.dynamic_slice_in_dim(own_offsets_all, start_at, blocks, 0)
        gap_leaves = (
            jnp.mod(leaf_ids[:, None] - name_rows + leaf_total // 2, leaf_total) - leaf_total // 2
        )
        kernel_tiles = tile_block(own_offsets, near_offsets, gap_leaves, spread).astype(
            jnp.bfloat16
        )
        return jnp.einsum(
            "lkab,lksb->lsa", kernel_tiles, near_values, preferred_element_type=jnp.float32
        )

    mapped = lax.map(near_block, jnp.arange(half_rows // blocks, dtype=jnp.int32))
    own_rows = mapped.reshape(half_rows, columns, points)
    kept_part = lax.dynamic_slice_in_dim(own_rows, side * samples, samples, 1)
    given_part = lax.dynamic_slice_in_dim(own_rows, (1 - side) * samples, samples, 1)
    received = swapped(given_part.astype(jnp.bfloat16), "sample", 0).astype(given_part.dtype)
    near_field = jnp.where(
        side == 0,
        jnp.concatenate([kept_part, received], axis=0),
        jnp.concatenate([received, kept_part], axis=0),
    )
    inverse = jnp.argsort(order, axis=1)
    natural_values = jnp.take_along_axis(basis, inverse[:, None, :], axis=2)
    expansion_weights = jnp.einsum(
        "ejt,ekt->ekj", natural_values, direction, preferred_element_type=jnp.float32
    ).astype(jnp.bfloat16)
    node_coef = jnp.einsum(
        "lrk,lsk->sr", leaf_transfer, expansion_weights, preferred_element_type=jnp.float32
    ).astype(jnp.bfloat16)
    lifted = jnp.einsum(
        "rk,sk->sr", node_transfer[0], node_coef, preferred_element_type=jnp.float32
    )
    top_node = lax.psum(lifted, "leaf").astype(jnp.bfloat16)
    every_top = lax.all_gather(top_node[None], "blk", axis=0, tiled=True)
    chosen = every_top[top_list[0]]
    incoming = jnp.einsum(
        "krj,ksj->sr", top_coupling[0], chosen, preferred_element_type=jnp.float32
    )
    incoming = incoming.astype(jnp.bfloat16)
    down_coef = jnp.einsum(
        "rk,sr->sk", node_transfer[0], incoming, preferred_element_type=jnp.float32
    ).astype(jnp.bfloat16)
    coef_wide = padded(expansion_weights, ((("blk", "leaf"), 0),), leaf_dev)
    paired_block = coef_wide[jnp.mod(coupling_list - (first_leaf - leaf_dev), leaf_total)]
    upward_gathered = jnp.einsum(
        "lrk,sr->lsk", leaf_transfer, down_coef, preferred_element_type=jnp.float32
    )
    upward_gathered = upward_gathered + jnp.einsum(
        "ohvd,ohgd->ogv", coupling, paired_block, preferred_element_type=jnp.float32
    )
    upward_gathered = upward_gathered.astype(jnp.bfloat16)
    distant_field = jnp.einsum(
        "bfw,baf->baw", natural_values, upward_gathered, preferred_element_type=jnp.float32
    )
    product_image = NUGGET * direction.astype(jnp.float32) + near_field + distant_field
    residual_next = residual - step[None, :, None] * product_image
    new_square = jnp.sum(residual_next * residual_next, axis=(0, 2))
    new_norm = lax.psum(new_square, ("blk", "leaf"))
    beta_ratio = new_norm / old_norm
    direction_next = (
        residual_next + beta_ratio[None, :, None] * direction.astype(jnp.float32)
    ).astype(jnp.bfloat16)
    return (residual_next, direction_next)


def solution(mesh):
    in_specs = (
        P(("groups", "blk", "leaf"), "sample", None),
        P(("groups", "blk", "leaf"), "sample", None),
        P(("groups", "sample")),
        P(("groups", "blk", "leaf"), None, None),
        P(("groups", "blk", "leaf"), None),
        P(("groups", "blk", "leaf"), None, None),
        P(("groups", "blk", "leaf"), None, None),
        P(("groups", "blk", "leaf"), None, None),
        P(("groups", "blk", "leaf"), None),
        P(("groups", "blk", "leaf"), None),
        P(("groups", "blk", "leaf"), None, None, None),
        P(("groups", "blk"), None),
        P(("groups", "blk"), None, None, None),
    )
    out_specs = (
        P(("groups", "blk", "leaf"), "sample", None),
        P(("groups", "blk", "leaf"), "sample", None),
    )
    return jax.shard_map(
        on_device, mesh=mesh, in_specs=in_specs, out_specs=out_specs, check_vma=False
    )
```

profile of v0, /device:TPU:0, one launch (start us, length us, event | category | flops | bytes accessed | tf_op | source)
XLA Modules:
  0.0 217.3 jit_solution(16189384715876912534)
XLA Ops:
  10.1 2.9 %collective-permute-start = (bf16[16,67,256]{2,0,1:T(8,128)(2,1)S(1)}, bf16[16,67,256]{2,0,1:T(8,128)(2,1)S(1)}, u32[]{:S(2)}, u32[]{:S(2)}) collective-permute-start(bf16[16,67,256]{2,0,1:T(8,128)(2,1)S(1)} %get-tuple-element.173), channel_id=1, source_target_pairs={{0,2},{2,4},{4,6},{6,8},{8,10},{10,12},{12,14},{14,0},{1,3},{3,5},... | collective-permute-start | bytes 1646600 | tf_op jit(solution)/shard_map/ppermute | solution.py:21
  13.1 3.0 %collective-permute-start.1 = (bf16[16,67,256]{2,0,1:T(8,128)(2,1)S(1)}, bf16[16,67,256]{2,0,1:T(8,128)(2,1)}, u32[]{:S(2)}, u32[]{:S(2)}) collective-permute-start(bf16[16,67,256]{2,0,1:T(8,128)(2,1)S(1)} %get-tuple-element.173), channel_id=1, source_target_pairs={{2,0},{4,2},{6,4},{8,6},{10,8},{12,10},{14,12},{0,14},{3,1},{5,3},... | collective-permute-start | bytes 1646600 | tf_op jit(solution)/shard_map/ppermute | solution.py:22
  17.6 1.9 multiply_reduce_fusion
  20.2 16.4 %collective-permute-done = bf16[16,67,256]{2,0,1:T(8,128)(2,1)S(1)} collective-permute-done((bf16[16,67,256]{2,0,1:T(8,128)(2,1)S(1)}, bf16[16,67,256]{2,0,1:T(8,128)(2,1)S(1)}, u32[]{:S(2)}, u32[]{:S(2)}) %collective-permute-start) | collective-permute-done | bytes 548896 | tf_op jit(solution)/shard_map/ppermute | solution.py:21
  36.5 2.3 %collective-permute-done.1 = bf16[16,67,256]{2,0,1:T(8,128)(2,1)} collective-permute-done((bf16[16,67,256]{2,0,1:T(8,128)(2,1)S(1)}, bf16[16,67,256]{2,0,1:T(8,128)(2,1)}, u32[]{:S(2)}, u32[]{:S(2)}) %collective-permute-start.1) | collective-permute-done | bytes 548896 | tf_op jit(solution)/shard_map/ppermute | solution.py:22
  45.4 40.6 %gather_fusion.4 = bf16[4096,64]{1,0:T(8,128)(2,1)} fusion(bf16[16,64,256]{1,2,0:T(8,128)(2,1)S(1)} %copy.38, s32[4096]{0:T(1024)S(1)} %bitcast.104), kind=kCustom, calls=%fused_computation.4 | custom fusion | bytes 1081344 | tf_op jit(solution)/shard_map/jit(take_along_axis)/gather | solution.py:119
  86.0 2.4 %copy.39 = bf16[16,256,64]{1,2,0:T(8,128)(2,1)} copy(bf16[16,256,64]{2,1,0:T(8,128)(2,1)} %bitcast.109) | data formatting | bytes 1048576 | tf_op jit(solution)/shard_map/jit(take_along_axis)/gather | solution.py:119
  88.4 2.2 %fusion.12 = bf16[16,64,64]{1,2,0:T(8,128)(2,1)} fusion(bf16[16,64,256]{2,1,0:T(8,128)(2,1)} %param.16, bf16[16,256,64]{1,2,0:T(8,128)(2,1)} %copy.39, pred[16,256]{1,0:T(8,128)(4,1)S(1)} %compare_and_fusion), kind=kOutput, calls=%fused_computation.37 | convolution fusion | flops 33882112 | bytes 1183744 | tf_op jit(solution)/shard_map/ejt,ekt->ekj/dot_general | solution.py:120
  91.0 4.3 %collective-permute-start.5 = (bf16[16,64,64]{1,2,0:T(8,128)(2,1)}, bf16[16,64,64]{1,2,0:T(8,128)(2,1)}, u32[]{:S(2)}, u32[]{:S(2)}) collective-permute-start(bf16[16,64,64]{1,2,0:T(8,128)(2,1)} %fusion.12), channel_id=1, source_target_pairs={{2,0},{4,2},{6,4},{8,6},{10,8},{12,10},{14,12},{0,14},{3,1},{5,3},... | collective-permute-start | bytes 393224 | tf_op jit(solution)/shard_map/ppermute | solution.py:22
  96.7 11.0 %psum.21 = bf16[64,64]{1,0:T(8,128)(2,1)S(1)} all-reduce(f32[64,64]{1,0:T(8,128)S(1)} %fusion.17), channel_id=1, replica_groups=mesh['groups'=2,'blk'=4,'leaf'=2,'sample'=2] {'leaf'}, use_global_device_ids=true, to_apply=%region_3.4 | all-reduce | flops 4096 | bytes 24576 | tf_op jit(solution)/shard_map/psum | solution.py:129
  107.7 13.5 %all-gather = bf16[256,64]{1,0:T(8,128)(2,1)S(1)} all-gather(bf16[64,64]{1,0:T(8,128)(2,1)S(1)} %psum.21), channel_id=2, replica_groups=mesh['groups'=2,'blk'=4,'leaf'=2,'sample'=2] {'blk'}, dimensions={0}, use_global_device_ids=true | all-gather | bytes 40960 | tf_op jit(solution)/shard_map/all_gather | solution.py:130
  124.5 3.1 %maximum_select_fusion = bf16[48,128,256]{2,0,1:T(8,128)(2,1)S(1)} fusion(bf16[48,64,256]{2,0,1:T(8,128)(2,1)} %collective-permute-done.2, bf16[48,64,256]{2,0,1:T(8,128)(2,1)} %slice.57, pred[]{:T(512)S(6)} %eq.12), kind=kLoop, calls=%fused_computation.28 | loop fusion | flops 4718592 | bytes 6291457 | tf_op jit(solution)/shard_map/jit(_where)/select_n | solution.py:81
  127.7 2.8 %copy.36 = bf16[48,128,256]{2,1,0:T(8,128)(2,1)} copy(bf16[48,128,256]{2,0,1:T(8,128)(2,1)S(1)} %maximum_select_fusion) | data formatting | bytes 6291456 | tf_op jit(solution)/shard_map/while | solution.py:108
  130.4 42.3 %while.12 = (s32[]{:T(128)}, f32[2,4,128,256]{3,2,1,0:T(8,128)}, s32[2]{0:T(128)S(1)}, s32[]{:T(128)}, s32[16,12]{1,0:T(8,128)}, /*index=5*/bf16[48,128,256]{2,1...) while((s32[]{:T(128)}, f32[2,4,128,256]{3,2,1,0:T(8,128)}, ...), condition=%wide.region_1.0_spmd, body=%wide.region_0.0_spmd.sunk | while | flops 852494208 | bytes 11184823 | solution.py:108
  134.2 4.4 %gather_fusion = bf16[48,128,256]{2,1,0:T(8,128)(2,1)} fusion(bf16[48,128,256]{2,1,0:T(8,128)(2,1)} %get-tuple-element.290, s32[1024]{0:T(1024)S(1)} %pad_clamp_fusion.4), kind=kCustom, calls=%fused_computation.clone.1 | custom fusion | bytes 6291648 | tf_op jit(solution)/shard_map/while/body/eval_jaxpr/gather | solution.py:95
  139.4 12.2 %fusion.54 = f32[2,4,128,256]{3,2,1,0:T(8,128)} fusion(f32[2,4,128,256]{3,2,1,0:T(8,128)} %get-tuple-element.270, s32[]{:T(128)} %get-tuple-element.269, bf16[4,12,128,256]{3,2,1,0:T(8,128)(2,1)} %bitcast.105, f32[4,12,256]{2,1,0:T(8,128)S(1)} %copy.62, f32[4,256]{1,0:T(4,128)S(1)} %get-tuple-element.248, f32[4,12,256]{2,1,0:T(8,128)S(1)} %copy.63, ...), kind=kOutput, calls=%fused_computation.8.clone.1 | convolution fusion | flops 852492288 | bytes 3830464 | tf_op jit(solution)/shard_map/while/body/eval_jaxpr/lkab,lksb->lsa/dot_general | solution.py:104
  155.4 4.4 %gather_fusion = bf16[48,128,256]{2,1,0:T(8,128)(2,1)} fusion(bf16[48,128,256]{2,1,0:T(8,128)(2,1)} %get-tuple-element.290, s32[1024]{0:T(1024)S(1)} %pad_clamp_fusion.4), kind=kCustom, calls=%fused_computation.clone.1 | custom fusion | bytes 6291648 | tf_op jit(solution)/shard_map/while/body/eval_jaxpr/gather | solution.py:95
  160.6 12.1 %fusion.54 = f32[2,4,128,256]{3,2,1,0:T(8,128)} fusion(f32[2,4,128,256]{3,2,1,0:T(8,128)} %get-tuple-element.270, s32[]{:T(128)} %get-tuple-element.269, bf16[4,12,128,256]{3,2,1,0:T(8,128)(2,1)} %bitcast.105, f32[4,12,256]{2,1,0:T(8,128)S(1)} %copy.62, f32[4,256]{1,0:T(4,128)S(1)} %get-tuple-element.248, f32[4,12,256]{2,1,0:T(8,128)S(1)} %copy.63, ...), kind=kOutput, calls=%fused_computation.8.clone.1 | convolution fusion | flops 852492288 | bytes 3830464 | tf_op jit(solution)/shard_map/while/body/eval_jaxpr/lkab,lksb->lsa/dot_general | solution.py:104
  172.7 1.8 dynamic-slice_convert_fusion
  176.8 2.1 gather_fusion.3
  179.0 1.9 constant_dynamic-slice_fusion
  181.9 4.6 %multiply_reduce_fusion.1 = (f32[64]{0:T(128)S(1)}, f32[16,64,256]{2,1,0:T(8,128)}) fusion(f32[16,64,256]{2,1,0:T(8,128)} %param.15, bf16[16,256,64]{1,2,0:T(8,128)(2,1)} %copy.39, pred[16,256]{1,0:T(8,128)(4,1)S(1)} %copy-done.12, f32[16,64,64]{2,1,0:T(8,128)} %convolution_bitcast_fusion.1, bf16[16,8,64,64]{2,3,1,0:T(8,128)(2,1)} %bitcast.107, ...), kind=kOutput, calls=%fused_computation.54 | convolution fusion | flops 103940032 | bytes 6558209 | tf_op jit(solution)/shard_map/bfw,baf->baw/dot_general | solution.py:148
  186.5 21.7 %all-reduce = (f32[64]{0:T(128)S(1)}, f32[64]{0:T(128)S(1)}) all-reduce(f32[64]{0:T(128)S(1)} %get-tuple-element.174, f32[64]{0:T(128)S(1)} %copy-done.14), channel_id=1, replica_groups=mesh['groups'=2,'blk'=4,'leaf'=2,'sample'=2] {'blk','leaf'}, use_global_device_ids=true, to_apply=%region_5.6 | all-reduce | flops 128 | bytes 1024 | tf_op jit(solution)/shard_map/psum | solution.py:154
  208.2 2.2 %fusion.23 = bf16[16,64,256]{2,1,0:T(8,128)(2,1)} fusion(f32[16,64,256]{2,1,0:T(8,128)} %get-tuple-element.175, bf16[16,64,256]{2,1,0:T(8,128)(2,1)S(1)} %copy-done.3, f32[64]{0:T(128)S(1)} %div.3), kind=kLoop, calls=%fused_computation.51 | loop fusion | flops 1048576 | bytes 2097408 | tf_op jit(solution)/shard_map/convert_element_type | solution.py:158
  (95 shorter events, 27.5 us)
Async XLA Ops:
  7.2 174.7 %copy-start = (bf16[16,8,64,64]{3,2,1,0:T(8,128)(2,1)S(1)}, bf16[16,8,64,64]{3,2,1,0:T(8,128)(2,1)}, u32[]{:S(2)}) copy-start(bf16[16,8,64,64]{3,2,1,0:T(8,128)(2,1)} %param.25) | copy-start | bytes 3145732
  7.2 37.5 %sort.19.cloned.1.call-start = ((), (), s32[]{:S(2)}) async-start(), calls=%async_computation | async-start | bytes 98336 | tf_op jit(solution)/shard_map/jit(argsort)/sort | solution.py:118
  10.1 31.2 %copy-start.1 = (bf16[16,67,256]{2,0,1:T(8,128)(2,1)}, bf16[16,67,256]{2,0,1:T(8,128)(2,1)S(1)}, u32[]{:S(2)}) copy-start(bf16[16,67,256]{2,0,1:T(8,128)(2,1)S(1)} %get-tuple-element.173) | copy-start | bytes 1646596
  10.1 26.4 %collective-permute-start = (bf16[16,67,256]{2,0,1:T(8,128)(2,1)S(1)}, bf16[16,67,256]{2,0,1:T(8,128)(2,1)S(1)}, u32[]{:S(2)}, u32[]{:S(2)}) collective-permute-start(bf16[16,67,256]{2,0,1:T(8,128)(2,1)S(1)} %get-tuple-element.173), channel_id=1, source_target_pairs={{0,2},{2,4},{4,6},{6,8},{8,10},{10,12},{12,14},{14,0},{1,3},{3,5},... | collective-permute-start | bytes 1646600 | tf_op jit(solution)/shard_map/ppermute | solution.py:21
  13.1 25.8 %collective-permute-start.1 = (bf16[16,67,256]{2,0,1:T(8,128)(2,1)S(1)}, bf16[16,67,256]{2,0,1:T(8,128)(2,1)}, u32[]{:S(2)}, u32[]{:S(2)}) collective-permute-start(bf16[16,67,256]{2,0,1:T(8,128)(2,1)S(1)} %get-tuple-element.173), channel_id=1, source_target_pairs={{2,0},{4,2},{6,4},{8,6},{10,8},{12,10},{14,12},{0,14},{3,1},{5,3},... | collective-permute-start | bytes 1646600 | tf_op jit(solution)/shard_map/ppermute | solution.py:22
  20.2 21.7 %copy-start.9 = (s32[16,12]{1,0:T(8,128)S(1)}, s32[16,12]{1,0:T(8,128)}, u32[]{:S(2)}) copy-start(s32[16,12]{1,0:T(8,128)} %param.23) | copy-start | bytes 2308
  36.5 4.8 %copy-start.4 = (bf16[16,67,256]{2,0,1:T(8,128)(2,1)}, bf16[16,67,256]{2,0,1:T(8,128)(2,1)S(1)}, u32[]{:S(2)}) copy-start(bf16[16,67,256]{2,0,1:T(8,128)(2,1)S(1)} %collective-permute-done) | copy-start | bytes 1646596
  41.3 83.2 %collective-permute-start.2 = (bf16[48,64,256]{2,0,1:T(8,128)(2,1)}, bf16[48,64,256]{2,0,1:T(8,128)(2,1)}, u32[]{:S(2)}, u32[]{:S(2)}) collective-permute-start(bf16[48,64,256]{2,0,1:T(8,128)(2,1)} %slice.57), channel_id=1, source_target_pairs={{0,1},{1,0},{2,3},{3,2},{4,5},{5,4},{6,7},{7,6},{8,9},{9,8},{10,11... | collective-permute-start | bytes 4718600 | tf_op jit(solution)/shard_map/ppermute | solution.py:28
  45.4 43.0 %copy-start.8 = (s32[16,256]{1,0:T(8,128)S(1)}, s32[16,256]{1,0:T(8,128)}, u32[]{:S(2)}) copy-start(s32[16,256]{1,0:T(8,128)} %get-tuple-element.131) | copy-start | bytes 49156
  45.4 50.0 %copy-start.7 = (bf16[1,64,64]{2,1,0:T(8,128)(2,1)S(1)}, bf16[1,64,64]{2,1,0:T(8,128)(2,1)}, u32[]{:S(2)}) copy-start(bf16[1,64,64]{2,1,0:T(8,128)(2,1)} %param.22) | copy-start | bytes 24580
  86.0 9.4 %copy-start.6 = (bf16[16,64,64]{2,1,0:T(8,128)(2,1)S(1)}, bf16[16,64,64]{2,1,0:T(8,128)(2,1)}, u32[]{:S(2)}) copy-start(bf16[16,64,64]{2,1,0:T(8,128)(2,1)} %param.21) | copy-start | bytes 393220
  86.0 37.7 %copy-start.2 = (bf16[16,67,256]{2,0,1:T(8,128)(2,1)S(1)}, bf16[16,67,256]{2,0,1:T(8,128)(2,1)}, u32[]{:S(2)}) copy-start(bf16[16,67,256]{2,0,1:T(8,128)(2,1)} %copy-done.1) | copy-start | bytes 1646596
  86.0 37.7 %copy-start.5 = (bf16[16,67,256]{2,0,1:T(8,128)(2,1)S(1)}, bf16[16,67,256]{2,0,1:T(8,128)(2,1)}, u32[]{:S(2)}) copy-start(bf16[16,67,256]{2,0,1:T(8,128)(2,1)} %copy-done.4) | copy-start | bytes 1646596
  88.4 2.6 %copy-start.11 = (pred[16,256]{1,0:T(8,128)(4,1)}, pred[16,256]{1,0:T(8,128)(4,1)S(1)}, u32[]{:S(2)}) copy-start(pred[16,256]{1,0:T(8,128)(4,1)S(1)} %compare_and_fusion) | copy-start | bytes 12292
  90.6 84.9 %collective-permute-start.4 = (bf16[16,64,64]{1,2,0:T(8,128)(2,1)}, bf16[16,64,64]{1,2,0:T(8,128)(2,1)}, u32[]{:S(2)}, u32[]{:S(2)}) collective-permute-start(bf16[16,64,64]{1,2,0:T(8,128)(2,1)} %fusion.12), channel_id=1, source_target_pairs={{0,2},{2,4},{4,6},{6,8},{8,10},{10,12},{12,14},{14,0},{1,3},{3,5},... | collective-permute-start | bytes 393224 | tf_op jit(solution)/shard_map/ppermute | solution.py:21
  91.0 84.5 %collective-permute-start.5 = (bf16[16,64,64]{1,2,0:T(8,128)(2,1)}, bf16[16,64,64]{1,2,0:T(8,128)(2,1)}, u32[]{:S(2)}, u32[]{:S(2)}) collective-permute-start(bf16[16,64,64]{1,2,0:T(8,128)(2,1)} %fusion.12), channel_id=1, source_target_pairs={{2,0},{4,2},{6,4},{8,6},{10,8},{12,10},{14,12},{0,14},{3,1},{5,3},... | collective-permute-start | bytes 393224 | tf_op jit(solution)/shard_map/ppermute | solution.py:22
  130.4 46.4 %copy-start.10 = (s32[1024]{0:T(1024)S(1)}, s32[1024]{0:T(1024)}, u32[]{:S(2)}) copy-start(s32[1024]{0:T(1024)} %pad_clamp_fusion.1) | copy-start | bytes 12292
  174.5 6.4 %collective-permute-start.3 = (bf16[8,64,256]{2,1,0:T(8,128)(2,1)}, bf16[8,64,256]{2,1,0:T(8,128)(2,1)}, u32[]{:S(2)}, u32[]{:S(2)}) collective-permute-start(bf16[8,64,256]{2,1,0:T(8,128)(2,1)} %dynamic-slice_convert_fusion), channel_id=1, source_target_pairs={{0,1},{1,0},{2,3},{3,2},{4,5},{5,4},{6,7},{7,6},{8,9},{9,8},{10,11... | collective-permute-start | bytes 786440 | tf_op jit(solution)/shard_map/ppermute | solution.py:28
  176.8 5.1 %copy-start.3 = (bf16[16,64,256]{2,1,0:T(8,128)(2,1)S(1)}, bf16[16,64,256]{2,1,0:T(8,128)(2,1)}, u32[]{:S(2)}) copy-start(bf16[16,64,256]{2,1,0:T(8,128)(2,1)} %param.16) | copy-start | bytes 1572868
  176.8 5.1 %copy-start.12 = (pred[16,256]{1,0:T(8,128)(4,1)S(1)}, pred[16,256]{1,0:T(8,128)(4,1)}, u32[]{:S(2)}) copy-start(pred[16,256]{1,0:T(8,128)(4,1)} %copy-done.11) | copy-start | bytes 12292
  176.8 5.1 %copy-start.13 = (f32[64]{0:T(128)S(1)}, f32[64]{0:T(128)}, u32[]{:S(2)}) copy-start(f32[64]{0:T(128)} %param.17) | copy-start | bytes 772
  181.9 4.6 %copy-start.14 = (f32[64]{0:T(128)S(1)}, f32[64]{0:T(128)}, u32[]{:S(2)}) copy-start(f32[64]{0:T(128)} %multiply_reduce_fusion) | copy-start | bytes 772
Sparse Core Ops, SparseCore 0:
  16.9 2.5 sort.21.cloned.1.call-done
  (1 shorter events, 0.0 us)
where the time goes:
time: 218 us; the launch traced here: 217 us
  local copies, waits for them, and re-layouts  71.6 us (33%)
  blocking collectives  46.2 us (21%)
  matrix products  34.6 us (16%)
  other arithmetic  19.7 us (9%)
  waiting for transfers between devices  18.7 us (9%)
  between operations  14.3 us (7%)
  starting transfers between devices  10.7 us (5%)
    gather x2, local copies, waits for them, and re-layouts, on_device(): natural_values = jnp.take_along_axis(basis, inverse[:, None, :], axis=2)  43 us
    dot_general x2, matrix products, near_block(): jnp.einsum('lkab,lksb->lsa', kernel_tiles, near_values, preferred_element...  24.3 us
    psum x1, blocking collectives, on_device(): new_norm = lax.psum(new_square, ('blk', 'leaf'))  21.7 us
    ppermute x2, waiting for transfers between devices, padded(): before = lax.ppermute(last, axis, up)  16.4 us
    all_gather x1, blocking collectives, on_device(): every_top = lax.all_gather(top_node[None], 'blk', axis=0, tiled=True)  13.5 us
    psum x1, blocking collectives, on_device(): top_node = lax.psum(lifted, 'leaf').astype(jnp.bfloat16)  11 us
    gather x2, local copies, waits for them, and re-layouts, near_block(): near_values = all_columns[slot_rows]  8.85 us
    ppermute x2, starting transfers between devices, padded(): after = lax.ppermute(initial, axis, down)  7.38 us
  transfers between devices with their start and end apart: 6, of which 2 were waited for; matrix products, arithmetic and copies ran while one was open for 52% of the time, Pallas kernels for 0%

commit v1 on v0

--- a/solution.py
+++ b/solution.py
@@ -58,6 +58,32 @@
     top_list,
     top_coupling,
 ):
+
+    def number_patch(my_tile, join_dim=0):
+        z1 = lax.axis_size("blk")
+        r_now = lax.axis_index("blk")
+        base_arr, b_next, w2 = (z1, r_now, my_tile.shape[join_dim])
+        column = tuple(((ix, (ix + 1) % base_arr) for ix in range(base_arr)))
+        seen = tuple(((ix, (ix - 1) % base_arr) for ix in range(base_arr)))
+        low = jnp.zeros(
+            (*my_tile.shape[:join_dim], base_arr * w2, *my_tile.shape[join_dim + 1 :]),
+            my_tile.dtype,
+        )
+        low = lax.dynamic_update_slice_in_dim(low, my_tile, b_next * w2, axis=join_dim)
+        then = current_value = my_tile
+        p_next = base_arr // 2
+        for jj in range(1, p_next + 1):
+            then = lax.ppermute(then, axis_name="blk", perm=column)
+            low = lax.dynamic_update_slice_in_dim(
+                low, then, (b_next - jj) % base_arr * w2, axis=join_dim
+            )
+            if jj < base_arr - p_next:
+                current_value = lax.ppermute(current_value, "blk", seen)
+                low = lax.dynamic_update_slice_in_dim(
+                    low, current_value, (b_next + jj) % base_arr * w2, axis=join_dim
+                )
+        return low
+
     leaf_dev = direction.shape[0]
     samples = direction.shape[1]
     points = direction.shape[2]
@@ -127,7 +153,7 @@
         "rk,sk->sr", node_transfer[0], node_coef, preferred_element_type=jnp.float32
     )
     top_node = lax.psum(lifted, "leaf").astype(jnp.bfloat16)
-    every_top = lax.all_gather(top_node[None], "blk", axis=0, tiled=True)
+    every_top = number_patch(top_node[None])
     chosen = every_top[top_list[0]]
     incoming = jnp.einsum(
         "krj,ksj->sr", top_coupling[0], chosen, preferred_element_type=jnp.float32

time: 218 us -> 201 us (0.922)
  blocking collectives: 46.2 us -> 24.3 us
  starting transfers between devices: 10.7 us -> 14.8 us
  waiting for transfers between devices: 18.7 us -> 20.9 us
    all_gather x1 -> x0, blocking collectives: 13.5 us -> none  [on_device(): every_top = lax.all_gather(top_node[None], 'blk', axis=0, tiled=True)]
    ppermute x0 -> x3, waiting for transfers between devices: none -> 5.48 us  [the longest x2 5.48 us: number_patch(): then = lax.ppermute(then, axis_name='blk', perm=column)]
    psum x1, blocking collectives: 21.7 us -> 17.1 us  [on_device(): new_norm = lax.psum(new_square, ('blk', 'leaf'))]
    ppermute x0 -> x3, starting transfers between devices: none -> 4.11 us  [the longest x1 2.25 us: number_patch(): current_value = lax.ppermute(current_value, 'blk', seen)]
    psum x1, blocking collectives: 11 us -> 7.15 us  [on_device(): top_node = lax.psum(lifted, 'leaf').astype(jnp.bfloat16)]
    ppermute x2, waiting for transfers between devices: 16.4 us -> 13.2 us  [padded(): before = lax.ppermute(last, axis, up)]
    unnamed x34 -> x28, local copies, waits for them, and re-layouts: 3.11 us -> 4.53 us
  transfers between devices with their start and end apart: 6 -> 9, of which waited for: 2 -> 3; matrix products, arithmetic and copies ran while one was open for 52% -> 55% of each run, Pallas kernels for 0% -> 0%
where the time goes in v1:
time: 201 us; the launch traced here: 200 us
  local copies, waits for them, and re-layouts  71.4 us (36%)
  matrix products  32.7 us (16%)
  blocking collectives  24.3 us (12%)
  waiting for transfers between devices  20.9 us (10%)
  other arithmetic  20 us (10%)
  starting transfers between devices  14.8 us (7%)
  between operations  14.4 us (7%)
    gather x2, local copies, waits for them, and re-layouts, on_device(): natural_values = jnp.take_along_axis(basis, inverse[:, None, :], axis=2)  42.1 us
    dot_general x2, matrix products, near_block(): jnp.einsum('lkab,lksb->lsa', kernel_tiles, near_values, preferred_element...  24.3 us
    psum x1, blocking collectives, on_device(): new_norm = lax.psum(new_square, ('blk', 'leaf'))  17.1 us
    ppermute x2, waiting for transfers between devices, padded(): before = lax.ppermute(last, axis, up)  13.2 us
    gather x2, local copies, waits for them, and re-layouts, near_block(): near_values = all_columns[slot_rows]  8.85 us
    psum x1, blocking collectives, on_device(): top_node = lax.psum(lifted, 'leaf').astype(jnp.bfloat16)  7.15 us
    ppermute x2, starting transfers between devices, padded(): after = lax.ppermute(initial, axis, down)  6.03 us
    ppermute x2, waiting for transfers between devices, number_patch(): then = lax.ppermute(then, axis_name='blk', perm=column)  5.48 us
  transfers between devices with their start and end apart: 9, of which 3 were waited for; matrix products, arithmetic and copies ran while one was open for 55% of the time, Pallas kernels for 0%

profile of v1, /device:TPU:0, one launch (start us, length us, event | category | flops | bytes accessed | tf_op | source)
XLA Modules:
  0.0 200.0 jit_solution(10416384587022324397)
XLA Ops:
  7.2 2.3 %copy_dynamic-update-slice_fusion = bf16[16,67,256]{2,0,1:T(8,128)(2,1)} fusion(bf16[16,64,256]{2,1,0:T(8,128)(2,1)} %param.16), kind=kLoop, calls=%fused_computation.56 | loop fusion | bytes 1048576
  11.0 2.9 %collective-permute-start = (bf16[16,67,256]{2,0,1:T(8,128)(2,1)}, bf16[16,67,256]{2,0,1:T(8,128)(2,1)}, u32[]{:S(2)}, u32[]{:S(2)}) collective-permute-start(bf16[16,67,256]{2,0,1:T(8,128)(2,1)} %get-tuple-element.173), channel_id=1, source_target_pairs={{0,2},{2,4},{4,6},{6,8},{8,10},{10,12},{12,14},{14,0},{1,3},{3,5},... | collective-permute-start | bytes 1646600 | tf_op jit(solution)/shard_map/ppermute | solution.py:21
  13.9 3.0 %collective-permute-start.1 = (bf16[16,67,256]{2,0,1:T(8,128)(2,1)}, bf16[16,67,256]{2,0,1:T(8,128)(2,1)}, u32[]{:S(2)}, u32[]{:S(2)}) collective-permute-start(bf16[16,67,256]{2,0,1:T(8,128)(2,1)} %get-tuple-element.173), channel_id=1, source_target_pairs={{2,0},{4,2},{6,4},{8,6},{10,8},{12,10},{14,12},{0,14},{3,1},{5,3},... | collective-permute-start | bytes 1646600 | tf_op jit(solution)/shard_map/ppermute | solution.py:22
  21.9 2.0 multiply_reduce_fusion
  24.5 13.2 %collective-permute-done = bf16[16,67,256]{2,0,1:T(8,128)(2,1)} collective-permute-done((bf16[16,67,256]{2,0,1:T(8,128)(2,1)}, bf16[16,67,256]{2,0,1:T(8,128)(2,1)}, u32[]{:S(2)}, u32[]{:S(2)}) %collective-permute-start) | collective-permute-done | bytes 548896 | tf_op jit(solution)/shard_map/ppermute | solution.py:21
  37.7 2.2 %collective-permute-done.1 = bf16[16,67,256]{2,0,1:T(8,128)(2,1)} collective-permute-done((bf16[16,67,256]{2,0,1:T(8,128)(2,1)}, bf16[16,67,256]{2,0,1:T(8,128)(2,1)}, u32[]{:S(2)}, u32[]{:S(2)}) %collective-permute-start.1) | collective-permute-done | bytes 548896 | tf_op jit(solution)/shard_map/ppermute | solution.py:22
  43.4 40.6 %gather_fusion.4 = bf16[4096,64]{1,0:T(8,128)(2,1)} fusion(bf16[16,64,256]{1,2,0:T(8,128)(2,1)S(1)} %copy.38, s32[4096]{0:T(1024)S(1)} %bitcast.107), kind=kCustom, calls=%fused_computation.4 | custom fusion | bytes 1081344 | tf_op jit(solution)/shard_map/jit(take_along_axis)/gather | solution.py:145
  88.0 7.2 %psum.21 = bf16[64,64]{1,0:T(8,128)(2,1)S(1)} all-reduce(f32[64,64]{1,0:T(8,128)S(1)} %fusion.17), channel_id=1, replica_groups=mesh['groups'=2,'blk'=4,'leaf'=2,'sample'=2] {'leaf'}, use_global_device_ids=true, to_apply=%region_3.4 | all-reduce | flops 4096 | bytes 24576 | tf_op jit(solution)/shard_map/psum | solution.py:155
  96.7 2.3 %collective-permute-start.5 = (bf16[1,64,64]{2,1,0:T(8,128)(2,1)S(1)}, bf16[1,64,64]{2,1,0:T(8,128)(2,1)S(1)}, u32[]{:S(2)}, u32[]{:S(2)}) collective-permute-start(bf16[1,64,64]{2,1,0:T(8,128)(2,1)S(1)} %bitcast.116), channel_id=1, source_target_pairs={{0,12},{4,0},{8,4},{12,8},{1,13},{5,1},{9,5},{13,9},{2,14},{6,2},{... | collective-permute-start | bytes 24584 | tf_op jit(solution)/shard_map/ppermute | solution.py:81
  100.7 3.0 %collective-permute-start.8 = (bf16[16,64,64]{1,2,0:T(8,128)(2,1)S(1)}, bf16[16,64,64]{1,2,0:T(8,128)(2,1)}, u32[]{:S(2)}, u32[]{:S(2)}) collective-permute-start(bf16[16,64,64]{1,2,0:T(8,128)(2,1)S(1)} %fusion.12), channel_id=1, source_target_pairs={{2,0},{4,2},{6,4},{8,6},{10,8},{12,10},{14,12},{0,14},{3,1},{5,3},... | collective-permute-start | bytes 393224 | tf_op jit(solution)/shard_map/ppermute | solution.py:22
  104.1 5.5 %collective-permute-done.6 = bf16[1,64,64]{2,1,0:T(8,128)(2,1)S(1)} collective-permute-done((bf16[1,64,64]{2,1,0:T(8,128)(2,1)S(1)}, bf16[1,64,64]{2,1,0:T(8,128)(2,1)S(1)}, u32[]{:S(2)}, u32[]{:S(2)}) %collective-permute-start.6) | collective-permute-done | bytes 8224 | tf_op jit(solution)/shard_map/ppermute | solution.py:76
  112.2 3.1 %maximum_select_fusion = bf16[48,128,256]{2,0,1:T(8,128)(2,1)S(1)} fusion(bf16[48,64,256]{2,0,1:T(8,128)(2,1)} %collective-permute-done.2, bf16[48,64,256]{2,0,1:T(8,128)(2,1)} %slice.57, pred[]{:T(512)S(6)} %eq.16), kind=kLoop, calls=%fused_computation.28 | loop fusion | flops 4718592 | bytes 6291457 | tf_op jit(solution)/shard_map/jit(_where)/select_n | solution.py:107
  115.3 2.8 %copy.36 = bf16[48,128,256]{2,1,0:T(8,128)(2,1)} copy(bf16[48,128,256]{2,0,1:T(8,128)(2,1)S(1)} %maximum_select_fusion) | data formatting | bytes 6291456 | tf_op jit(solution)/shard_map/while | solution.py:134
  118.1 42.0 %while.12 = (s32[]{:T(128)}, f32[2,4,128,256]{3,2,1,0:T(8,128)}, s32[2]{0:T(128)S(1)}, s32[]{:T(128)}, s32[16,12]{1,0:T(8,128)}, /*index=5*/bf16[48,128,256]{2,1...) while((s32[]{:T(128)}, f32[2,4,128,256]{3,2,1,0:T(8,128)}, ...), condition=%wide.region_1.0_spmd, body=%wide.region_0.0_spmd.sunk | while | flops 852494208 | bytes 11184823 | solution.py:134
  121.8 4.4 %gather_fusion = bf16[48,128,256]{2,1,0:T(8,128)(2,1)} fusion(bf16[48,128,256]{2,1,0:T(8,128)(2,1)} %get-tuple-element.290, s32[1024]{0:T(1024)S(1)} %pad_clamp_fusion.4), kind=kCustom, calls=%fused_computation.clone.1 | custom fusion | bytes 6291648 | tf_op jit(solution)/shard_map/while/body/eval_jaxpr/gather | solution.py:121
  127.0 12.2 %fusion.54 = f32[2,4,128,256]{3,2,1,0:T(8,128)} fusion(f32[2,4,128,256]{3,2,1,0:T(8,128)} %get-tuple-element.270, s32[]{:T(128)} %get-tuple-element.269, bf16[4,12,128,256]{3,2,1,0:T(8,128)(2,1)} %bitcast.108, f32[4,12,256]{2,1,0:T(8,128)S(1)} %copy.62, f32[4,256]{1,0:T(4,128)S(1)} %get-tuple-element.248, f32[4,12,256]{2,1,0:T(8,128)S(1)} %copy.63, ...), kind=kOutput, calls=%fused_computation.8.clone.1 | convolution fusion | flops 852492288 | bytes 3830464 | tf_op jit(solution)/shard_map/while/body/eval_jaxpr/lkab,lksb->lsa/dot_general | solution.py:130
  142.8 4.4 %gather_fusion = bf16[48,128,256]{2,1,0:T(8,128)(2,1)} fusion(bf16[48,128,256]{2,1,0:T(8,128)(2,1)} %get-tuple-element.290, s32[1024]{0:T(1024)S(1)} %pad_clamp_fusion.4), kind=kCustom, calls=%fused_computation.clone.1 | custom fusion | bytes 6291648 | tf_op jit(solution)/shard_map/while/body/eval_jaxpr/gather | solution.py:121
  148.0 12.1 %fusion.54 = f32[2,4,128,256]{3,2,1,0:T(8,128)} fusion(f32[2,4,128,256]{3,2,1,0:T(8,128)} %get-tuple-element.270, s32[]{:T(128)} %get-tuple-element.269, bf16[4,12,128,256]{3,2,1,0:T(8,128)(2,1)} %bitcast.108, f32[4,12,256]{2,1,0:T(8,128)S(1)} %copy.62, f32[4,256]{1,0:T(4,128)S(1)} %get-tuple-element.248, f32[4,12,256]{2,1,0:T(8,128)S(1)} %copy.63, ...), kind=kOutput, calls=%fused_computation.8.clone.1 | convolution fusion | flops 852492288 | bytes 3830464 | tf_op jit(solution)/shard_map/while/body/eval_jaxpr/lkab,lksb->lsa/dot_general | solution.py:130
  160.1 1.8 dynamic-slice_convert_fusion
  164.1 2.1 %gather_fusion.3 = bf16[128,64,64]{1,2,0:T(8,128)(2,1)} fusion(bf16[48,64,64]{1,2,0:T(8,128)(2,1)S(1)} %pad_maximum_fusion.1, s32[1024]{0:T(1024)S(1)} %copy-done.7), kind=kCustom, calls=%fused_computation.3 | custom fusion | bytes 2097664 | tf_op jit(solution)/shard_map/gather | solution.py:166
  166.3 1.9 constant_dynamic-slice_fusion
  169.2 4.6 %multiply_reduce_fusion.1 = (f32[64]{0:T(128)S(1)}, f32[16,64,256]{2,1,0:T(8,128)}) fusion(f32[16,64,256]{2,1,0:T(8,128)} %param.15, bf16[16,256,64]{1,2,0:T(8,128)(2,1)} %copy-done.2, pred[16,256]{1,0:T(8,128)(4,1)S(1)} %copy-done.9, f32[16,64,64]{2,1,0:T(8,128)} %convolution_bitcast_fusion.1, bf16[16,8,64,64]{2,3,1,0:T(8,128)(2,1)} %bitcast.110, ...), kind=kOutput, calls=%fused_computation.54 | convolution fusion | flops 103940032 | bytes 6558209 | tf_op jit(solution)/shard_map/bfw,baf->baw/dot_general | solution.py:174
  173.8 17.1 %all-reduce = (f32[64]{0:T(128)S(1)}, f32[64]{0:T(128)S(1)}) all-reduce(f32[64]{0:T(128)S(1)} %get-tuple-element.174, f32[64]{0:T(128)S(1)} %copy-done.11), channel_id=1, replica_groups=mesh['groups'=2,'blk'=4,'leaf'=2,'sample'=2] {'blk','leaf'}, use_global_device_ids=true, to_apply=%region_5.6 | all-reduce | flops 128 | bytes 1024 | tf_op jit(solution)/shard_map/psum | solution.py:180
  190.9 2.2 %fusion.23 = bf16[16,64,256]{2,1,0:T(8,128)(2,1)} fusion(f32[16,64,256]{2,1,0:T(8,128)} %get-tuple-element.175, bf16[16,64,256]{2,1,0:T(8,128)(2,1)S(1)} %copy-done.1, f32[64]{0:T(128)S(1)} %div.3), kind=kLoop, calls=%fused_computation.51 | loop fusion | flops 1048576 | bytes 2097408 | tf_op jit(solution)/shard_map/convert_element_type | solution.py:184
  (99 shorter events, 31.3 us)
Async XLA Ops:
  7.2 162.0 %copy-start = (bf16[16,8,64,64]{3,2,1,0:T(8,128)(2,1)S(1)}, bf16[16,8,64,64]{3,2,1,0:T(8,128)(2,1)}, u32[]{:S(2)}) copy-start(bf16[16,8,64,64]{3,2,1,0:T(8,128)(2,1)} %param.25) | copy-start | bytes 3145732
  7.2 16.7 %copy-start.6 = (s32[16,12]{1,0:T(8,128)S(1)}, s32[16,12]{1,0:T(8,128)}, u32[]{:S(2)}) copy-start(s32[16,12]{1,0:T(8,128)} %param.23) | copy-start | bytes 2308
  7.2 35.5 %sort.19.cloned.1.call-start = ((), (), s32[]{:S(2)}) async-start(), calls=%async_computation | async-start | bytes 98336 | tf_op jit(solution)/shard_map/jit(argsort)/sort | solution.py:144
  11.0 26.7 %collective-permute-start = (bf16[16,67,256]{2,0,1:T(8,128)(2,1)}, bf16[16,67,256]{2,0,1:T(8,128)(2,1)}, u32[]{:S(2)}, u32[]{:S(2)}) collective-permute-start(bf16[16,67,256]{2,0,1:T(8,128)(2,1)} %get-tuple-element.173), channel_id=1, source_target_pairs={{0,2},{2,4},{4,6},{6,8},{8,10},{10,12},{12,14},{14,0},{1,3},{3,5},... | collective-permute-start | bytes 1646600 | tf_op jit(solution)/shard_map/ppermute | solution.py:21
  13.9 26.0 %collective-permute-start.1 = (bf16[16,67,256]{2,0,1:T(8,128)(2,1)}, bf16[16,67,256]{2,0,1:T(8,128)(2,1)}, u32[]{:S(2)}, u32[]{:S(2)}) collective-permute-start(bf16[16,67,256]{2,0,1:T(8,128)(2,1)} %get-tuple-element.173), channel_id=1, source_target_pairs={{2,0},{4,2},{6,4},{8,6},{10,8},{12,10},{14,12},{0,14},{3,1},{5,3},... | collective-permute-start | bytes 1646600 | tf_op jit(solution)/shard_map/ppermute | solution.py:22
  42.7 69.6 %collective-permute-start.2 = (bf16[48,64,256]{2,0,1:T(8,128)(2,1)}, bf16[48,64,256]{2,0,1:T(8,128)(2,1)}, u32[]{:S(2)}, u32[]{:S(2)}) collective-permute-start(bf16[48,64,256]{2,0,1:T(8,128)(2,1)} %slice.57), channel_id=1, source_target_pairs={{0,1},{1,0},{2,3},{3,2},{4,5},{5,4},{6,7},{7,6},{8,9},{9,8},{10,11... | collective-permute-start | bytes 4718600 | tf_op jit(solution)/shard_map/ppermute | solution.py:28
  43.4 42.2 %copy-start.5 = (s32[16,256]{1,0:T(8,128)S(1)}, s32[16,256]{1,0:T(8,128)}, u32[]{:S(2)}) copy-start(s32[16,256]{1,0:T(8,128)} %get-tuple-element.131) | copy-start | bytes 49156
  43.4 44.2 %copy-start.4 = (bf16[1,64,64]{2,1,0:T(8,128)(2,1)S(1)}, bf16[1,64,64]{2,1,0:T(8,128)(2,1)}, u32[]{:S(2)}) copy-start(bf16[1,64,64]{2,1,0:T(8,128)(2,1)} %param.22) | copy-start | bytes 24580
  84.0 3.6 %copy-start.3 = (bf16[16,64,64]{2,1,0:T(8,128)(2,1)S(1)}, bf16[16,64,64]{2,1,0:T(8,128)(2,1)}, u32[]{:S(2)}) copy-start(bf16[16,64,64]{2,1,0:T(8,128)(2,1)} %param.21) | copy-start | bytes 393220
  85.6 25.8 %copy-start.2 = (bf16[16,256,64]{1,2,0:T(8,128)(2,1)}, bf16[16,256,64]{1,2,0:T(8,128)(2,1)S(1)}, u32[]{:S(2)}) copy-start(bf16[16,256,64]{1,2,0:T(8,128)(2,1)S(1)} %copy.39) | copy-start | bytes 1572868
  85.6 0.6 copy-start.8
  95.1 8.6 %collective-permute-start.4 = (bf16[1,64,64]{2,1,0:T(8,128)(2,1)S(1)}, bf16[1,64,64]{2,1,0:T(8,128)(2,1)S(1)}, u32[]{:S(2)}, u32[]{:S(2)}) collective-permute-start(bf16[1,64,64]{2,1,0:T(8,128)(2,1)S(1)} %bitcast.115), channel_id=1, source_target_pairs={{0,4},{4,8},{8,12},{12,0},{1,5},{5,9},{9,13},{13,1},{2,6},{6,10},{... | collective-permute-start | bytes 24584 | tf_op jit(solution)/shard_map/ppermute | solution.py:76
  96.7 7.3 %collective-permute-start.5 = (bf16[1,64,64]{2,1,0:T(8,128)(2,1)S(1)}, bf16[1,64,64]{2,1,0:T(8,128)(2,1)S(1)}, u32[]{:S(2)}, u32[]{:S(2)}) collective-permute-start(bf16[1,64,64]{2,1,0:T(8,128)(2,1)S(1)} %bitcast.116), channel_id=1, source_target_pairs={{0,12},{4,0},{8,4},{12,8},{1,13},{5,1},{9,5},{13,9},{2,14},{6,2},{... | collective-permute-start | bytes 24584 | tf_op jit(solution)/shard_map/ppermute | solution.py:81
  99.0 63.9 %collective-permute-start.7 = (bf16[16,64,64]{1,2,0:T(8,128)(2,1)S(1)}, bf16[16,64,64]{1,2,0:T(8,128)(2,1)S(1)}, u32[]{:S(2)}, u32[]{:S(2)}) collective-permute-start(bf16[16,64,64]{1,2,0:T(8,128)(2,1)S(1)} %fusion.12), channel_id=1, source_target_pairs={{0,2},{2,4},{4,6},{6,8},{8,10},{10,12},{12,14},{14,0},{1,3},{3,5},... | collective-permute-start | bytes 393224 | tf_op jit(solution)/shard_map/ppermute | solution.py:21
  100.7 62.2 %collective-permute-start.8 = (bf16[16,64,64]{1,2,0:T(8,128)(2,1)S(1)}, bf16[16,64,64]{1,2,0:T(8,128)(2,1)}, u32[]{:S(2)}, u32[]{:S(2)}) collective-permute-start(bf16[16,64,64]{1,2,0:T(8,128)(2,1)S(1)} %fusion.12), channel_id=1, source_target_pairs={{2,0},{4,2},{6,4},{8,6},{10,8},{12,10},{14,12},{0,14},{3,1},{5,3},... | collective-permute-start | bytes 393224 | tf_op jit(solution)/shard_map/ppermute | solution.py:22
  103.8 5.8 %collective-permute-start.6 = (bf16[1,64,64]{2,1,0:T(8,128)(2,1)S(1)}, bf16[1,64,64]{2,1,0:T(8,128)(2,1)S(1)}, u32[]{:S(2)}, u32[]{:S(2)}) collective-permute-start(bf16[1,64,64]{2,1,0:T(8,128)(2,1)S(1)} %collective-permute-done.4), channel_id=1, source_target_pairs={{0,4},{4,8},{8,12},{12,0},{1,5},{5,9},{9,13},{13,1},{2,6},{6,10},{... | collective-permute-start | bytes 24584 | tf_op jit(solution)/shard_map/ppermute | solution.py:76
  118.1 46.0 %copy-start.7 = (s32[1024]{0:T(1024)S(1)}, s32[1024]{0:T(1024)}, u32[]{:S(2)}) copy-start(s32[1024]{0:T(1024)} %pad_clamp_fusion.1) | copy-start | bytes 12292
  161.9 6.2 %collective-permute-start.3 = (bf16[8,64,256]{2,1,0:T(8,128)(2,1)}, bf16[8,64,256]{2,1,0:T(8,128)(2,1)}, u32[]{:S(2)}, u32[]{:S(2)}) collective-permute-start(bf16[8,64,256]{2,1,0:T(8,128)(2,1)} %dynamic-slice_convert_fusion), channel_id=1, source_target_pairs={{0,1},{1,0},{2,3},{3,2},{4,5},{5,4},{6,7},{7,6},{8,9},{9,8},{10,11... | collective-permute-start | bytes 786440 | tf_op jit(solution)/shard_map/ppermute | solution.py:28
  164.1 5.1 %copy-start.1 = (bf16[16,64,256]{2,1,0:T(8,128)(2,1)S(1)}, bf16[16,64,256]{2,1,0:T(8,128)(2,1)}, u32[]{:S(2)}) copy-start(bf16[16,64,256]{2,1,0:T(8,128)(2,1)} %param.16) | copy-start | bytes 1572868
  164.1 5.1 %copy-start.9 = (pred[16,256]{1,0:T(8,128)(4,1)S(1)}, pred[16,256]{1,0:T(8,128)(4,1)}, u32[]{:S(2)}) copy-start(pred[16,256]{1,0:T(8,128)(4,1)} %copy-done.8) | copy-start | bytes 12292
  164.1 5.1 %copy-start.10 = (f32[64]{0:T(128)S(1)}, f32[64]{0:T(128)}, u32[]{:S(2)}) copy-start(f32[64]{0:T(128)} %param.17) | copy-start | bytes 772
  169.2 4.6 %copy-start.11 = (f32[64]{0:T(128)S(1)}, f32[64]{0:T(128)}, u32[]{:S(2)}) copy-start(f32[64]{0:T(128)} %multiply_reduce_fusion) | copy-start | bytes 772
Sparse Core Ops, SparseCore 0:
  17.7 2.5 sort.21.cloned.1.call-done
  (1 shorter events, 0.0 us)
